TPU v7x, 256 devices: a whole 4x4x8 slice. The times are simulated.
256 devices in a mesh: seq: 64 (over y, z, core), head: 4 (over x).
Axes of the slice: x: 4, y: 4, z: 8, core: 2. Of those that a mesh axis runs over, the one named last changes fastest.
Arguments:
- tokens: bfloat16 [16384, 2048], P('seq')
- w_qkv: bfloat16 [2048, 3, 2048], P(None, None, 'head'), may hold values from -0.125 to 0.125
- w_out: bfloat16 [2048, 2048], P('head'), may hold values from -0.125 to 0.125
- norm_gain: float32 [2048], replicated, may hold values from 0.25 to 1.75
- w_label: bfloat16 [2048, 128], replicated, may hold values from -0.125 to 0.125
- offset_mid: int32 [16], P('head'), may hold values from 0 to 7
- offset_far: int32 [16], P('head'), may hold values from 0 to 63
Outputs:
- logits: float32 [16384, 128], P('seq')
All inputs are finite; a program needn't handle non-finite values.
Results may differ from a plain program's by a relative error of at most 0.023.
The roundings to bfloat16 on the way count: a program that leaves them out, or rounds other values in their place, can miss the bound.
Values may be sent and summed in bfloat16 or wider, within the bound.
No kernel may reach another device: no remote copies, remote signals or barrier semaphores. Data moves between devices by JAX's collectives and lax.ppermute only.
A program may use at most 64 MiB of HBM per device.

v0:
```python
import jax
import jax.numpy as jnp
from jax import lax
from jax.sharding import PartitionSpec as P

SPAN = 8


def from_behind(block, axis, distance):
    devices = range(lax.axis_size(axis))
    route = [((i - distance) % len(devices), i) for i in devices]
    return lax.ppermute(block, axis, route)


def attend(queries, keys, values):
    scores = jnp.einsum(
        "rhe,she->hrs", queries, keys, preferred_element_type=jnp.float32
    ) / jnp.sqrt(jnp.float32(queries.shape[2]))
    top = jnp.max(scores, axis=-1)
    weights = jnp.exp(scores - top[..., None])
    total = jnp.sum(weights, axis=-1)
    summed = jnp.einsum(
        "hrs,she->rhe", weights.astype(jnp.bfloat16), values, preferred_element_type=jnp.float32
    )
    return (top.T, total.T, summed)


def select_rows(array, offsets, rate):
    rows = array.shape[0] // rate
    shaped = array.reshape(rows, rate, array.shape[1], array.shape[2])
    index = jnp.broadcast_to(
        offsets[None, None, :, None], (rows, 1, array.shape[1], array.shape[2])
    )
    return jnp.take_along_axis(shaped, index, axis=1)[:, 0]


def spread_rows(parts, offsets, rate):
    top, total, summed = parts
    rows = top.shape[0]
    marks = jnp.arange(rate, dtype=jnp.int32)[None, :, None] == offsets[None, None, :]
    top_full = jnp.where(marks, top[:, None, :], jnp.float32(-1e30)).reshape(rows * rate, -1)
    total_full = jnp.where(marks, total[:, None, :], jnp.float32(0.0)).reshape(rows * rate, -1)
    sum_full = jnp.where(marks[..., None], summed[:, None], jnp.float32(0.0)).reshape(
        rows * rate, summed.shape[1], summed.shape[2]
    )
    return (top_full, total_full, sum_full)


def body(tokens, w_qkv, w_out, norm_gain, w_label, offset_mid, offset_far):
    tok_rows = tokens.shape[0]
    local_heads = offset_mid.shape[0]
    head_size = w_qkv.shape[2] // local_heads
    qkv = jnp.einsum("td,dce->tce", tokens, w_qkv, preferred_element_type=jnp.float32).astype(
        jnp.bfloat16
    )
    qkv = qkv.reshape(tok_rows, 3, local_heads, head_size)
    queries, keys, values = (qkv[:, 0], qkv[:, 1], qkv[:, 2])
    seq_count = lax.axis_size("seq")
    near = attend(queries, keys, values)
    mid_q = select_rows(queries, offset_mid, SPAN)
    mid_kv = jnp.stack(
        [select_rows(keys, offset_mid, SPAN), select_rows(values, offset_mid, SPAN)], axis=0
    )
    mid_rows = mid_kv.shape[1]
    position = (lax.axis_index("seq") + SPAN // 2) % SPAN
    lower_pieces = []
    upper_pieces = []
    for step_back in range(1, SPAN):
        lower_pieces.insert(0, from_behind(mid_kv, "seq", step_back))
        upper_pieces.append(from_behind(mid_kv, "seq", -step_back))
    window = jnp.concatenate(lower_pieces + [mid_kv] + upper_pieces, axis=1)
    gathered = lax.dynamic_slice_in_dim(
        window, (SPAN - 1 - position) * mid_rows, SPAN * mid_rows, 1
    )
    middle = spread_rows(attend(mid_q, gathered[0], gathered[1]), offset_mid, SPAN)
    far_q = select_rows(queries, offset_far, seq_count)
    far_kv = jnp.stack(
        [select_rows(keys, offset_far, seq_count), select_rows(values, offset_far, seq_count)],
        axis=0,
    )
    far_all = lax.all_gather(far_kv, "seq", axis=1, tiled=True)
    distant = spread_rows(attend(far_q, far_all[0], far_all[1]), offset_far, seq_count)
    branches = [near, middle, distant]
    peak = jnp.maximum(jnp.maximum(near[0], middle[0]), distant[0])
    upper = jnp.zeros((tok_rows, local_heads, head_size), jnp.float32)
    lower = jnp.zeros((tok_rows, local_heads), jnp.float32)
    for top, total, summed in branches:
        factor = jnp.exp(top - peak)
        upper = upper + factor[..., None] * summed
        lower = lower + factor * total
    attn = (
        (upper / lower[..., None]).astype(jnp.bfloat16).reshape(tok_rows, local_heads * head_size)
    )
    partial_out = jnp.dot(attn, w_out, preferred_element_type=jnp.float32)
    projected = lax.psum(partial_out.astype(jnp.bfloat16), "head").astype(jnp.float32)
    mixed = tokens.astype(jnp.float32) + projected
    mean_sq = jnp.mean(mixed * mixed, axis=-1)
    scaled = (mixed * norm_gain).astype(jnp.bfloat16)
    product = jnp.dot(scaled, w_label, preferred_element_type=jnp.float32)
    return product / jnp.sqrt(mean_sq + 1e-05)[:, None]


def solution(mesh):
    return jax.shard_map(
        body,
        mesh=mesh,
        in_specs=(
            P("seq", None),
            P(None, None, "head"),
            P("head", None),
            P(),
            P(),
            P("head"),
            P("head"),
        ),
        out_specs=P("seq", None),
        check_vma=False,
    )
```

profile of v0, /device:TPU:8, one launch (start us, length us, event | category | flops | bytes accessed | tf_op | source)
XLA Modules:
  0.0 969.6 jit_solution(3699433661671569265)
XLA Ops:
  6.5 5.9 convolution_convert_fusion.1
  12.5 1.7 reshape.163
  16.3 235.5 %gather_fusion.1 = bf16[16384]{0:T(1024)(128)(2,1)} fusion(bf16[32,8,4,128]{3,1,0,2:T(8,128)(2,1)S(1)} %get-tuple-element.34, s32[16384]{0:T(1024)S(1)} %bitcast.149), kind=kCustom, calls=%fused_computation.2.clone | custom fusion | bytes 327680 | tf_op jit(solution)/shard_map/jit(take_along_axis)/gather | solution.py:34
  251.7 236.4 %gather_fusion.2 = bf16[16384]{0:T(1024)(128)(2,1)} fusion(bf16[32,8,4,128]{3,1,0,2:T(8,128)(2,1)S(1)} %get-tuple-element.20, s32[16384]{0:T(1024)S(1)} %bitcast.150), kind=kCustom, calls=%fused_computation.3.clone | custom fusion | bytes 327680 | tf_op jit(solution)/shard_map/jit(take_along_axis)/gather | solution.py:34
  489.6 4.1 collective-permute-start
  493.6 4.0 collective-permute-start.1
  498.0 3.2 collective-permute-start.3
  501.2 2.6 collective-permute-start.4
  503.8 2.2 fusion.59
  508.1 236.0 %gather_fusion = bf16[16384]{0:T(1024)(128)(2,1)} fusion(bf16[32,8,4,128]{3,1,0,2:T(8,128)(2,1)S(1)} %bitcast.152, s32[16384]{0:T(1024)S(1)} %bitcast.151), kind=kCustom, calls=%fused_computation.clone | custom fusion | bytes 327680 | tf_op jit(solution)/shard_map/jit(take_along_axis)/gather | solution.py:34
  744.2 22.2 %gather_fusion.5 = bf16[2048]{0:T(1024)(128)(2,1)S(1)} fusion(bf16[4,64,4,128]{3,1,0,2:T(8,128)(2,1)S(1)} %bitcast.158, s32[2048]{0:T(1024)S(1)} %bitcast.154), kind=kCustom, calls=%fused_computation.5.clone | custom fusion | bytes 40960 | tf_op jit(solution)/shard_map/jit(take_along_axis)/gather | solution.py:34
  766.4 22.2 %gather_fusion.4 = bf16[2048]{0:T(1024)(128)(2,1)S(1)} fusion(bf16[4,64,4,128]{3,1,0,2:T(8,128)(2,1)S(1)} %bitcast.157, s32[2048]{0:T(1024)S(1)} %bitcast.155), kind=kCustom, calls=%fused_computation.4.clone | custom fusion | bytes 40960 | tf_op jit(solution)/shard_map/jit(take_along_axis)/gather | solution.py:34
  788.6 22.2 %gather_fusion.3 = bf16[2048]{0:T(1024)(128)(2,1)S(1)} fusion(bf16[4,64,4,128]{3,1,0,2:T(8,128)(2,1)S(1)} %bitcast.153, s32[2048]{0:T(1024)S(1)} %bitcast.156), kind=kCustom, calls=%fused_computation.1.clone | custom fusion | bytes 40960 | tf_op jit(solution)/shard_map/jit(take_along_axis)/gather | solution.py:34
  810.8 48.7 %all_gather.3 = bf16[2,256,4,128]{3,2,0,1:T(4,128)(2,1)S(1)} all-gather(bf16[2,4,4,128]{3,2,0,1:T(4,128)(2,1)S(1)} %copy.67), channel_id=1, replica_groups=mesh['seq'=64,'head'=4] {'seq'}, dimensions={1}, use_global_device_ids=true | all-gather | bytes 532480 | tf_op jit(solution)/shard_map/all_gather | solution.py:81
  864.4 2.0 copy.73
  869.5 3.9 collective-permute-start.7
  878.2 1.7 collective-permute-start.11
  879.9 5.6 collective-permute-start.12
  887.9 6.6 collective-permute-done.12
  899.2 2.0 copy.71
  903.6 1.7 convolution_convert_fusion
  905.4 52.9 %all-reduce.2.cloned.1.call-done = bf16[256,2048]{1,0:T(8,128)(2,1)} async-done(((bf16[256,2048]{1,0:T(8,128)(2,1)}), bf16[256,2048]{1,0:T(8,128)(2,1)}) %all-reduce.2.cloned.1.call-update) | async-done | bytes 1048592 | tf_op jit(solution)/shard_map/psum | solution.py:95
  958.2 2.0 multiply_reduce_fusion
  960.2 2.5 convolution_divide_fusion
  (113 shorter events, 28.2 us)
Async XLA Ops:
  6.5 897.1 %copy-start = (bf16[512,2048]{1,0:T(8,128)(2,1)S(1)}, bf16[512,2048]{1,0:T(8,128)(2,1)}, u32[]{:S(2)}) copy-start(bf16[512,2048]{1,0:T(8,128)(2,1)} %param.13) | copy-start | bytes 6291460
  6.5 8.7 copy-start.9
  6.5 951.7 %all-reduce.2.cloned.1.call-start = ((), (), s32[]{:S(2)}) async-start(), calls=%async_computation | async-start | bytes 2097152 | tf_op jit(solution)/shard_map/psum | solution.py:95
  15.2 472.9 %copy-start.8 = (s32[4]{0:T(128)}, s32[4]{0:T(128)S(1)}, u32[]{:S(2)}) copy-start(s32[4]{0:T(128)S(1)} %broadcast_add_fusion.1) | copy-start | bytes 52
  15.8 472.3 %copy-start.7 = (pred[4]{0:T(512)(128)(4,1)}, pred[4]{0:T(512)(128)(4,1)S(1)}, u32[]{:S(2)}) copy-start(pred[4]{0:T(512)(128)(4,1)S(1)} %get-tuple-element.36) | copy-start | bytes 16
  251.7 252.0 %copy-start.2 = (bf16[256,1,4,128]{3,2,0,1:T(4,128)(2,1)S(1)}, bf16[256,1,4,128]{3,2,0,1:T(4,128)(2,1)}, u32[]{:S(2)}) copy-start(bf16[256,1,4,128]{3,2,0,1:T(4,128)(2,1)} %get-tuple-element.12) | copy-start | bytes 786436
  489.6 376.8 %collective-permute-start = (bf16[2,32,4,128]{3,1,2,0:T(8,128)(2,1)}, bf16[2,32,4,128]{3,1,2,0:T(8,128)(2,1)}, u32[]{:S(2)}, u32[]{:S(2)}) collective-permute-start(bf16[2,32,4,128]{3,1,2,0:T(8,128)(2,1)} %pad_maximum_fusion), channel_id=1, source_target_pairs={{228,0},{232,4},{236,8},{240,12},{244,16},{248,20},{252,24},{0,28}... | collective-permute-start | bytes 196616 | tf_op jit(solution)/shard_map/ppermute | solution.py:12
  493.6 374.9 %collective-permute-start.1 = (bf16[2,32,4,128]{3,1,2,0:T(8,128)(2,1)}, bf16[2,32,4,128]{3,1,2,0:T(8,128)(2,1)}, u32[]{:S(2)}, u32[]{:S(2)}) collective-permute-start(bf16[2,32,4,128]{3,1,2,0:T(8,128)(2,1)} %pad_maximum_fusion), channel_id=1, source_target_pairs={{232,0},{236,4},{240,8},{244,12},{248,16},{252,20},{0,24},{4,28},{... | collective-permute-start | bytes 196616 | tf_op jit(solution)/shard_map/ppermute | solution.py:12
  497.7 371.8 %collective-permute-start.2 = (bf16[2,32,4,128]{3,1,2,0:T(8,128)(2,1)}, bf16[2,32,4,128]{3,1,2,0:T(8,128)(2,1)}, u32[]{:S(2)}, u32[]{:S(2)}) collective-permute-start(bf16[2,32,4,128]{3,1,2,0:T(8,128)(2,1)} %pad_maximum_fusion), channel_id=1, source_target_pairs={{236,0},{240,4},{244,8},{248,12},{252,16},{0,20},{4,24},{8,28},{12... | collective-permute-start | bytes 196616 | tf_op jit(solution)/shard_map/ppermute | solution.py:12
  498.0 376.3 %collective-permute-start.3 = (bf16[2,32,4,128]{3,1,2,0:T(8,128)(2,1)}, bf16[2,32,4,128]{3,1,2,0:T(8,128)(2,1)}, u32[]{:S(2)}, u32[]{:S(2)}) collective-permute-start(bf16[2,32,4,128]{3,1,2,0:T(8,128)(2,1)} %pad_maximum_fusion), channel_id=1, source_target_pairs={{240,0},{244,4},{248,8},{252,12},{0,16},{4,20},{8,24},{12,28},{16,... | collective-permute-start | bytes 196616 | tf_op jit(solution)/shard_map/ppermute | solution.py:12
  501.2 374.8 %collective-permute-start.4 = (bf16[2,32,4,128]{3,1,2,0:T(8,128)(2,1)}, bf16[2,32,4,128]{3,1,2,0:T(8,128)(2,1)}, u32[]{:S(2)}, u32[]{:S(2)}) collective-permute-start(bf16[2,32,4,128]{3,1,2,0:T(8,128)(2,1)} %pad_maximum_fusion), channel_id=1, source_target_pairs={{244,0},{248,4},{252,8},{0,12},{4,16},{8,20},{12,24},{16,28},{20,3... | collective-permute-start | bytes 196616 | tf_op jit(solution)/shard_map/ppermute | solution.py:12
  508.1 236.0 %copy-start.10 = (pred[4]{0:T(512)(128)(4,1)S(1)}, pred[4]{0:T(512)(128)(4,1)}, u32[]{:S(2)}) copy-start(pred[4]{0:T(512)(128)(4,1)} %get-tuple-element.35) | copy-start | bytes 16
  788.6 71.4 %copy-start.1 = (f32[4,256,256]{1,2,0:T(8,128)S(1)}, f32[4,256,256]{1,2,0:T(8,128)}, u32[]{:S(2)}) copy-start(f32[4,256,256]{1,2,0:T(8,128)} %get-tuple-element.32) | copy-start | bytes 3145732
  866.4 10.5 %collective-permute-start.5 = (bf16[2,32,4,128]{3,1,2,0:T(8,128)(2,1)}, bf16[2,32,4,128]{3,1,2,0:T(8,128)(2,1)S(1)}, u32[]{:S(2)}, u32[]{:S(2)}) collective-permute-start(bf16[2,32,4,128]{3,1,2,0:T(8,128)(2,1)} %pad_maximum_fusion), channel_id=1, source_target_pairs={{248,0},{252,4},{0,8},{4,12},{8,16},{12,20},{16,24},{20,28},{24,32... | collective-permute-start | bytes 196616 | tf_op jit(solution)/shard_map/ppermute | solution.py:12
  868.5 9.7 collective-permute-start.6
  869.5 10.4 %collective-permute-start.7 = (bf16[2,32,4,128]{3,1,2,0:T(8,128)(2,1)}, bf16[2,32,4,128]{3,1,2,0:T(8,128)(2,1)S(1)}, u32[]{:S(2)}, u32[]{:S(2)}) collective-permute-start(bf16[2,32,4,128]{3,1,2,0:T(8,128)(2,1)} %pad_maximum_fusion), channel_id=1, source_target_pairs={{4,0},{8,4},{12,8},{16,12},{20,16},{24,20},{28,24},{32,28},{36,32}... | collective-permute-start | bytes 196616 | tf_op jit(solution)/shard_map/ppermute | solution.py:12
  874.2 11.2 %collective-permute-start.8 = (bf16[2,32,4,128]{3,1,2,0:T(8,128)(2,1)}, bf16[2,32,4,128]{3,1,2,0:T(8,128)(2,1)S(1)}, u32[]{:S(2)}, u32[]{:S(2)}) collective-permute-start(bf16[2,32,4,128]{3,1,2,0:T(8,128)(2,1)} %pad_maximum_fusion), channel_id=1, source_target_pairs={{8,0},{12,4},{16,8},{20,12},{24,16},{28,20},{32,24},{36,28},{40,32... | collective-permute-start | bytes 196616 | tf_op jit(solution)/shard_map/ppermute | solution.py:12
  875.9 10.4 %collective-permute-start.9 = (bf16[2,32,4,128]{3,1,2,0:T(8,128)(2,1)}, bf16[2,32,4,128]{3,1,2,0:T(8,128)(2,1)S(1)}, u32[]{:S(2)}, u32[]{:S(2)}) collective-permute-start(bf16[2,32,4,128]{3,1,2,0:T(8,128)(2,1)} %pad_maximum_fusion), channel_id=1, source_target_pairs={{12,0},{16,4},{20,8},{24,12},{28,16},{32,20},{36,24},{40,28},{44,3... | collective-permute-start | bytes 196616 | tf_op jit(solution)/shard_map/ppermute | solution.py:12
  876.9 9.9 %collective-permute-start.10 = (bf16[2,32,4,128]{3,1,2,0:T(8,128)(2,1)}, bf16[2,32,4,128]{3,1,2,0:T(8,128)(2,1)S(1)}, u32[]{:S(2)}, u32[]{:S(2)}) collective-permute-start(bf16[2,32,4,128]{3,1,2,0:T(8,128)(2,1)} %pad_maximum_fusion), channel_id=1, source_target_pairs={{16,0},{20,4},{24,8},{28,12},{32,16},{36,20},{40,24},{44,28},{48,3... | collective-permute-start | bytes 196616 | tf_op jit(solution)/shard_map/ppermute | solution.py:12
  878.2 9.7 %collective-permute-start.11 = (bf16[2,32,4,128]{3,1,2,0:T(8,128)(2,1)}, bf16[2,32,4,128]{3,1,2,0:T(8,128)(2,1)S(1)}, u32[]{:S(2)}, u32[]{:S(2)}) collective-permute-start(bf16[2,32,4,128]{3,1,2,0:T(8,128)(2,1)} %pad_maximum_fusion), channel_id=1, source_target_pairs={{20,0},{24,4},{28,8},{32,12},{36,16},{40,20},{44,24},{48,28},{52,3... | collective-permute-start | bytes 196616 | tf_op jit(solution)/shard_map/ppermute | solution.py:12
  879.9 14.6 %collective-permute-start.12 = (bf16[2,32,4,128]{3,1,2,0:T(8,128)(2,1)}, bf16[2,32,4,128]{3,1,2,0:T(8,128)(2,1)S(1)}, u32[]{:S(2)}, u32[]{:S(2)}) collective-permute-start(bf16[2,32,4,128]{3,1,2,0:T(8,128)(2,1)} %pad_maximum_fusion), channel_id=1, source_target_pairs={{24,0},{28,4},{32,8},{36,12},{40,16},{44,20},{48,24},{52,28},{56,3... | collective-permute-start | bytes 196616 | tf_op jit(solution)/shard_map/ppermute | solution.py:12
  885.5 9.1 collective-permute-start.13
  897.1 63.1 %copy-start.11 = (f32[2048]{0:T(1024)S(1)}, f32[2048]{0:T(1024)}, u32[]{:S(2)}) copy-start(f32[2048]{0:T(1024)} %param.14) | copy-start | bytes 24580
  903.6 56.6 %copy-start.4 = (bf16[256,2048]{1,0:T(8,128)(2,1)S(1)}, bf16[256,2048]{1,0:T(8,128)(2,1)}, u32[]{:S(2)}) copy-start(bf16[256,2048]{1,0:T(8,128)(2,1)} %param.11) | copy-start | bytes 3145732
  (3 other events, 10.5 us)
Sparse Core Ops, SparseCore 0:
  905.5 52.6 all-reduce.1
where the time goes:
time: 970 us
  local copies, waits for them, and re-layouts  793 us (82%)
  waiting for transfers between devices  61.1 us (6%)
  blocking collectives  48.7 us (5%)
  starting transfers between devices  29.6 us (3%)
  matrix products  16.8 us (2%)
  between operations  13.7 us (1%)
    gather x7, local copies, waits for them, and re-layouts, select_rows(): return jnp.take_along_axis(shaped, index, axis=1)[:, 0]  774 us
    psum x1, waiting for transfers between devices, body(): lax.psum(partial_out.astype(jnp.bfloat16), 'head').astype(jnp.float32)  52.9 us
    all_gather x1, blocking collectives, body(): far_all = lax.all_gather(far_kv, 'seq', axis=1, tiled=True)  48.7 us
    ppermute x14, starting transfers between devices, from_behind(): return lax.ppermute(block, axis, route)  29.6 us
  transfers between devices with their start and end apart: 15, of which 5 were waited for; matrix products, arithmetic and copies ran while one was open for 33% of the time, Pallas kernels for 0%

commit v1 on v0

--- a/solution.py
+++ b/solution.py
@@ -78,7 +78,8 @@
         [select_rows(keys, offset_far, seq_count), select_rows(values, offset_far, seq_count)],
         axis=0,
     )
-    far_all = lax.all_gather(far_kv, "seq", axis=1, tiled=True)
+    stack = jnp.stack([far_kv] * lax.axis_size("seq"))
+    far_all = jnp.concatenate(lax.all_to_all(stack, "seq", 0, 0), axis=1)
     distant = spread_rows(attend(far_q, far_all[0], far_all[1]), offset_far, seq_count)
     branches = [near, middle, distant]
     peak = jnp.maximum(jnp.maximum(near[0], middle[0]), distant[0])

time: 970 us -> 787 us (0.81)
  local copies, waits for them, and re-layouts: 793 us -> 650 us
  blocking collectives: 48.7 us -> 0 us
  starting transfers between devices: 29.6 us -> 40.9 us
    gather x7, local copies, waits for them, and re-layouts: 774 us -> 630 us  [select_rows(): return jnp.take_along_axis(shaped, index, axis=1)[:, 0]]
    all_gather x1 -> x0, blocking collectives: 48.7 us -> none  [body(): far_all = lax.all_gather(far_kv, 'seq', axis=1, tiled=True)]
  transfers between devices with their start and end apart: 15 -> 16, of which waited for: 5 -> 3; matrix products, arithmetic and copies ran while one was open for 33% -> 41% of each run, Pallas kernels for 0% -> 0%
where the time goes in v1:
time: 787 us; the launch traced here: 786 us
  local copies, waits for them, and re-layouts  650 us (83%)
  waiting for transfers between devices  58.5 us (7%)
  starting transfers between devices  40.9 us (5%)
  matrix products  15.9 us (2%)
  between operations  13.9 us (2%)
    gather x7, local copies, waits for them, and re-layouts, select_rows(): return jnp.take_along_axis(shaped, index, axis=1)[:, 0]  630 us
    psum x1, waiting for transfers between devices, body(): lax.psum(partial_out.astype(jnp.bfloat16), 'head').astype(jnp.float32)  52.4 us
    ppermute x14, starting transfers between devices, from_behind(): return lax.ppermute(block, axis, route)  33.1 us
  transfers between devices with their start and end apart: 16, of which 3 were waited for; matrix products, arithmetic and copies ran while one was open for 41% of the time, Pallas kernels for 0%

profile of v1, /device:TPU:8, one launch (start us, length us, event | category | flops | bytes accessed | tf_op | source)
XLA Modules:
  0.0 785.8 jit_solution(10798245600985077650)
XLA Ops:
  6.5 5.9 convolution_convert_fusion.1
  12.5 1.7 reshape.173
  16.4 163.7 %gather_fusion.1 = bf16[16384]{0:T(1024)(128)(2,1)S(1)} fusion(bf16[32,8,4,128]{3,1,0,2:T(8,128)(2,1)S(1)} %get-tuple-element.34, s32[16384]{0:T(1024)S(1)} %bitcast.146), kind=kCustom, calls=%fused_computation.2.clone | custom fusion | bytes 327680 | tf_op jit(solution)/shard_map/jit(take_along_axis)/gather | solution.py:34
  180.1 163.7 %gather_fusion.2 = bf16[16384]{0:T(1024)(128)(2,1)S(1)} fusion(bf16[32,8,4,128]{3,1,0,2:T(8,128)(2,1)S(1)} %get-tuple-element.20, s32[16384]{0:T(1024)S(1)} %bitcast.147), kind=kCustom, calls=%fused_computation.3.clone | custom fusion | bytes 327680 | tf_op jit(solution)/shard_map/jit(take_along_axis)/gather | solution.py:34
  344.6 4.1 collective-permute-start
  348.6 4.0 collective-permute-start.1
  352.9 3.2 collective-permute-start.3
  356.1 2.6 collective-permute-start.4
  359.6 22.2 %gather_fusion.5 = bf16[2048]{0:T(1024)(128)(2,1)S(1)} fusion(bf16[4,64,4,128]{3,1,0,2:T(8,128)(2,1)S(1)} %bitcast.155, s32[2048]{0:T(1024)S(1)} %bitcast.151), kind=kCustom, calls=%fused_computation.5.clone | custom fusion | bytes 40960 | tf_op jit(solution)/shard_map/jit(take_along_axis)/gather | solution.py:34
  381.7 22.2 %gather_fusion.4 = bf16[2048]{0:T(1024)(128)(2,1)S(1)} fusion(bf16[4,64,4,128]{3,1,0,2:T(8,128)(2,1)S(1)} %bitcast.154, s32[2048]{0:T(1024)S(1)} %bitcast.152), kind=kCustom, calls=%fused_computation.4.clone | custom fusion | bytes 40960 | tf_op jit(solution)/shard_map/jit(take_along_axis)/gather | solution.py:34
  403.9 22.2 %gather_fusion.3 = bf16[2048]{0:T(1024)(128)(2,1)S(1)} fusion(bf16[4,64,4,128]{3,1,0,2:T(8,128)(2,1)S(1)} %bitcast.149, s32[2048]{0:T(1024)S(1)} %bitcast.153), kind=kCustom, calls=%fused_computation.1.clone | custom fusion | bytes 40960 | tf_op jit(solution)/shard_map/jit(take_along_axis)/gather | solution.py:34
  427.1 7.5 all-to-all-start
  437.7 1.8 copy.69
  439.5 236.0 %gather_fusion = bf16[16384]{0:T(1024)(128)(2,1)} fusion(bf16[32,8,4,128]{3,1,0,2:T(8,128)(2,1)S(1)} %bitcast.150, s32[16384]{0:T(1024)S(1)} %bitcast.148), kind=kCustom, calls=%fused_computation.clone | custom fusion | bytes 327680 | tf_op jit(solution)/shard_map/jit(take_along_axis)/gather | solution.py:34
  680.4 3.9 collective-permute-start.7
  687.6 3.4 collective-permute-start.10
  692.6 4.2 collective-permute-start.12
  696.8 3.7 collective-permute-start.13
  701.0 5.7 collective-permute-done.13
  711.3 2.0 copy.63
  716.6 2.0 copy.65
  722.0 52.4 %all-reduce.2.cloned.1.call-done = bf16[256,2048]{1,0:T(8,128)(2,1)} async-done(((bf16[256,2048]{1,0:T(8,128)(2,1)}), bf16[256,2048]{1,0:T(8,128)(2,1)}) %all-reduce.2.cloned.1.call-update) | async-done | bytes 1048592 | tf_op jit(solution)/shard_map/psum | solution.py:96
  774.4 2.0 multiply_reduce_fusion
  776.4 2.5 convolution_divide_fusion
  (117 shorter events, 29.3 us)
Async XLA Ops:
  6.5 713.8 %copy-start = (bf16[512,2048]{1,0:T(8,128)(2,1)S(1)}, bf16[512,2048]{1,0:T(8,128)(2,1)}, u32[]{:S(2)}) copy-start(bf16[512,2048]{1,0:T(8,128)(2,1)} %param.13) | copy-start | bytes 6291460
  6.5 8.7 %copy-start.9 = (s32[4]{0:T(128)S(1)}, s32[4]{0:T(128)}, u32[]{:S(2)}) copy-start(s32[4]{0:T(128)} %param.17) | copy-start | bytes 52
  15.2 328.6 %copy-start.8 = (s32[4]{0:T(128)}, s32[4]{0:T(128)S(1)}, u32[]{:S(2)}) copy-start(s32[4]{0:T(128)S(1)} %broadcast_add_fusion.1) | copy-start | bytes 52
  15.9 327.9 %copy-start.7 = (pred[4]{0:T(512)(128)(4,1)}, pred[4]{0:T(512)(128)(4,1)S(1)}, u32[]{:S(2)}) copy-start(pred[4]{0:T(512)(128)(4,1)S(1)} %get-tuple-element.36) | copy-start | bytes 16
  180.1 178.6 %copy-start.2 = (bf16[256,1,4,128]{3,2,0,1:T(4,128)(2,1)S(1)}, bf16[256,1,4,128]{3,2,0,1:T(4,128)(2,1)}, u32[]{:S(2)}) copy-start(bf16[256,1,4,128]{3,2,0,1:T(4,128)(2,1)} %get-tuple-element.12) | copy-start | bytes 786436
  344.6 332.6 %collective-permute-start = (bf16[2,32,4,128]{3,1,2,0:T(8,128)(2,1)}, bf16[2,32,4,128]{3,1,2,0:T(8,128)(2,1)}, u32[]{:S(2)}, u32[]{:S(2)}) collective-permute-start(bf16[2,32,4,128]{3,1,2,0:T(8,128)(2,1)} %pad_maximum_fusion), channel_id=1, source_target_pairs={{228,0},{232,4},{236,8},{240,12},{244,16},{248,20},{252,24},{0,28}... | collective-permute-start | bytes 196616 | tf_op jit(solution)/shard_map/ppermute | solution.py:12
  348.6 330.8 %collective-permute-start.1 = (bf16[2,32,4,128]{3,1,2,0:T(8,128)(2,1)}, bf16[2,32,4,128]{3,1,2,0:T(8,128)(2,1)}, u32[]{:S(2)}, u32[]{:S(2)}) collective-permute-start(bf16[2,32,4,128]{3,1,2,0:T(8,128)(2,1)} %pad_maximum_fusion), channel_id=1, source_target_pairs={{232,0},{236,4},{240,8},{244,12},{248,16},{252,20},{0,24},{4,28},{... | collective-permute-start | bytes 196616 | tf_op jit(solution)/shard_map/ppermute | solution.py:12
  352.7 327.7 %collective-permute-start.2 = (bf16[2,32,4,128]{3,1,2,0:T(8,128)(2,1)}, bf16[2,32,4,128]{3,1,2,0:T(8,128)(2,1)}, u32[]{:S(2)}, u32[]{:S(2)}) collective-permute-start(bf16[2,32,4,128]{3,1,2,0:T(8,128)(2,1)} %pad_maximum_fusion), channel_id=1, source_target_pairs={{236,0},{240,4},{244,8},{248,12},{252,16},{0,20},{4,24},{8,28},{12... | collective-permute-start | bytes 196616 | tf_op jit(solution)/shard_map/ppermute | solution.py:12
  352.9 332.2 %collective-permute-start.3 = (bf16[2,32,4,128]{3,1,2,0:T(8,128)(2,1)}, bf16[2,32,4,128]{3,1,2,0:T(8,128)(2,1)}, u32[]{:S(2)}, u32[]{:S(2)}) collective-permute-start(bf16[2,32,4,128]{3,1,2,0:T(8,128)(2,1)} %pad_maximum_fusion), channel_id=1, source_target_pairs={{240,0},{244,4},{248,8},{252,12},{0,16},{4,20},{8,24},{12,28},{16,... | collective-permute-start | bytes 196616 | tf_op jit(solution)/shard_map/ppermute | solution.py:12
  356.1 330.5 %collective-permute-start.4 = (bf16[2,32,4,128]{3,1,2,0:T(8,128)(2,1)}, bf16[2,32,4,128]{3,1,2,0:T(8,128)(2,1)}, u32[]{:S(2)}, u32[]{:S(2)}) collective-permute-start(bf16[2,32,4,128]{3,1,2,0:T(8,128)(2,1)} %pad_maximum_fusion), channel_id=1, source_target_pairs={{244,0},{248,4},{252,8},{0,12},{4,16},{8,20},{12,24},{16,28},{20,3... | collective-permute-start | bytes 196616 | tf_op jit(solution)/shard_map/ppermute | solution.py:12
  381.7 44.3 %copy-start.10 = (pred[4]{0:T(512)(128)(4,1)S(1)}, pred[4]{0:T(512)(128)(4,1)}, u32[]{:S(2)}) copy-start(pred[4]{0:T(512)(128)(4,1)} %get-tuple-element.35) | copy-start | bytes 16
  427.1 286.2 %all-to-all-start = ((bf16[64,2,4,4,128]{4,2,3,1,0:T(4,128)(2,1)}), bf16[64,2,4,4,128]{4,2,3,1,0:T(4,128)(2,1)}, u32[]{:S(2)}, u32[]{:S(2)}) async-start(bf16[64,2,4,4,128]{4,2,3,1,0:T(4,128)(2,1)} %stack.8), calls=%async_computation | async-start | bytes 1048576 | tf_op jit(solution)/shard_map/all_to_all | solution.py:82
  434.7 339.7 %all-reduce.2.cloned.1.call-start = ((), (), s32[]{:S(2)}) async-start(), calls=%async_computation.1 | async-start | bytes 2097152 | tf_op jit(solution)/shard_map/psum | solution.py:96
  677.1 10.5 %collective-permute-start.5 = (bf16[2,32,4,128]{3,1,2,0:T(8,128)(2,1)}, bf16[2,32,4,128]{3,1,2,0:T(8,128)(2,1)S(1)}, u32[]{:S(2)}, u32[]{:S(2)}) collective-permute-start(bf16[2,32,4,128]{3,1,2,0:T(8,128)(2,1)} %pad_maximum_fusion), channel_id=1, source_target_pairs={{248,0},{252,4},{0,8},{4,12},{8,16},{12,20},{16,24},{20,28},{24,32... | collective-permute-start | bytes 196616 | tf_op jit(solution)/shard_map/ppermute | solution.py:12
  679.4 11.6 %collective-permute-start.6 = (bf16[2,32,4,128]{3,1,2,0:T(8,128)(2,1)}, bf16[2,32,4,128]{3,1,2,0:T(8,128)(2,1)S(1)}, u32[]{:S(2)}, u32[]{:S(2)}) collective-permute-start(bf16[2,32,4,128]{3,1,2,0:T(8,128)(2,1)} %pad_maximum_fusion), channel_id=1, source_target_pairs={{252,0},{0,4},{4,8},{8,12},{12,16},{16,20},{20,24},{24,28},{28,32}... | collective-permute-start | bytes 196616 | tf_op jit(solution)/shard_map/ppermute | solution.py:12
  680.4 12.2 %collective-permute-start.7 = (bf16[2,32,4,128]{3,1,2,0:T(8,128)(2,1)}, bf16[2,32,4,128]{3,1,2,0:T(8,128)(2,1)S(1)}, u32[]{:S(2)}, u32[]{:S(2)}) collective-permute-start(bf16[2,32,4,128]{3,1,2,0:T(8,128)(2,1)} %pad_maximum_fusion), channel_id=1, source_target_pairs={{4,0},{8,4},{12,8},{16,12},{20,16},{24,20},{28,24},{32,28},{36,32}... | collective-permute-start | bytes 196616 | tf_op jit(solution)/shard_map/ppermute | solution.py:12
  685.2 11.7 %collective-permute-start.8 = (bf16[2,32,4,128]{3,1,2,0:T(8,128)(2,1)}, bf16[2,32,4,128]{3,1,2,0:T(8,128)(2,1)S(1)}, u32[]{:S(2)}, u32[]{:S(2)}) collective-permute-start(bf16[2,32,4,128]{3,1,2,0:T(8,128)(2,1)} %pad_maximum_fusion), channel_id=1, source_target_pairs={{8,0},{12,4},{16,8},{20,12},{24,16},{28,20},{32,24},{36,28},{40,32... | collective-permute-start | bytes 196616 | tf_op jit(solution)/shard_map/ppermute | solution.py:12
  686.7 13.9 %collective-permute-start.9 = (bf16[2,32,4,128]{3,1,2,0:T(8,128)(2,1)}, bf16[2,32,4,128]{3,1,2,0:T(8,128)(2,1)S(1)}, u32[]{:S(2)}, u32[]{:S(2)}) collective-permute-start(bf16[2,32,4,128]{3,1,2,0:T(8,128)(2,1)} %pad_maximum_fusion), channel_id=1, source_target_pairs={{12,0},{16,4},{20,8},{24,12},{28,16},{32,20},{36,24},{40,28},{44,3... | collective-permute-start | bytes 196616 | tf_op jit(solution)/shard_map/ppermute | solution.py:12
  687.6 12.9 %collective-permute-start.10 = (bf16[2,32,4,128]{3,1,2,0:T(8,128)(2,1)}, bf16[2,32,4,128]{3,1,2,0:T(8,128)(2,1)S(1)}, u32[]{:S(2)}, u32[]{:S(2)}) collective-permute-start(bf16[2,32,4,128]{3,1,2,0:T(8,128)(2,1)} %pad_maximum_fusion), channel_id=1, source_target_pairs={{16,0},{20,4},{24,8},{28,12},{32,16},{36,20},{40,24},{44,28},{48,3... | collective-permute-start | bytes 196616 | tf_op jit(solution)/shard_map/ppermute | solution.py:12
  691.0 9.6 %collective-permute-start.11 = (bf16[2,32,4,128]{3,1,2,0:T(8,128)(2,1)}, bf16[2,32,4,128]{3,1,2,0:T(8,128)(2,1)S(1)}, u32[]{:S(2)}, u32[]{:S(2)}) collective-permute-start(bf16[2,32,4,128]{3,1,2,0:T(8,128)(2,1)} %pad_maximum_fusion), channel_id=1, source_target_pairs={{20,0},{24,4},{28,8},{32,12},{36,16},{40,20},{44,24},{48,28},{52,3... | collective-permute-start | bytes 196616 | tf_op jit(solution)/shard_map/ppermute | solution.py:12
  692.6 8.4 %collective-permute-start.12 = (bf16[2,32,4,128]{3,1,2,0:T(8,128)(2,1)}, bf16[2,32,4,128]{3,1,2,0:T(8,128)(2,1)S(1)}, u32[]{:S(2)}, u32[]{:S(2)}) collective-permute-start(bf16[2,32,4,128]{3,1,2,0:T(8,128)(2,1)} %pad_maximum_fusion), channel_id=1, source_target_pairs={{24,0},{28,4},{32,8},{36,12},{40,16},{44,20},{48,24},{52,28},{56,3... | collective-permute-start | bytes 196616 | tf_op jit(solution)/shard_map/ppermute | solution.py:12
  696.8 9.8 %collective-permute-start.13 = (bf16[2,32,4,128]{3,1,2,0:T(8,128)(2,1)}, bf16[2,32,4,128]{3,1,2,0:T(8,128)(2,1)S(1)}, u32[]{:S(2)}, u32[]{:S(2)}) collective-permute-start(bf16[2,32,4,128]{3,1,2,0:T(8,128)(2,1)} %pad_maximum_fusion), channel_id=1, source_target_pairs={{28,0},{32,4},{36,8},{40,12},{44,16},{48,20},{52,24},{56,28},{60,3... | collective-permute-start | bytes 196616 | tf_op jit(solution)/shard_map/ppermute | solution.py:12
  715.4 61.0 %copy-start.11 = (f32[2048]{0:T(1024)S(1)}, f32[2048]{0:T(1024)}, u32[]{:S(2)}) copy-start(f32[2048]{0:T(1024)} %param.14) | copy-start | bytes 24580
  720.3 56.1 %copy-start.4 = (bf16[256,2048]{1,0:T(8,128)(2,1)S(1)}, bf16[256,2048]{1,0:T(8,128)(2,1)}, u32[]{:S(2)}) copy-start(bf16[256,2048]{1,0:T(8,128)(2,1)} %param.11) | copy-start | bytes 3145732
  (4 other events, 11.7 us)
Sparse Core Ops, SparseCore 0:
  722.2 52.1 all-reduce.1
